TPU v7x, 256 devices: a whole 4x4x8 slice. The times are simulated.
256 devices in a mesh: seq: 8 (over y, core), tensor: 32 (over z, x).
Axes of the slice: x: 4, y: 4, z: 8, core: 2. Of those that a mesh axis runs over, the one named last changes fastest.
Arguments:
- tokens: bfloat16 [4096, 3584], P('seq', 'tensor'), may hold values from -6 to 6
- w_zx: bfloat16 [2, 3584, 4096], P(None, None, 'tensor'), may hold values from -0.09375 to 0.09375
- w_bc: bfloat16 [3584, 128], replicated, may hold values from -0.09375 to 0.09375
- w_dt: bfloat16 [3584, 64], P(None, 'tensor'), may hold values from -0.09375 to 0.09375
- dt_bias: float32 [64], P('tensor'), may hold values from -2 to 0.5
- a_rate: float32 [64], P('tensor'), may hold values from 0.00012207031 to 0.05
- d_skip: float32 [64], P('tensor'), may hold values from 0.3 to 1.5
- conv_x: float32 [4, 4096], P(None, 'tensor'), may hold values from -3 to 3
- conv_bc: float32 [4, 128], replicated, may hold values from -3 to 3
- norm_gain: float32 [4096], P('tensor'), may hold values from 0.25 to 1.75
- w_out: bfloat16 [4096, 3584], P('tensor'), may hold values from -0.09375 to 0.09375
- segments: int32 [4096], P('seq'), may hold values from 0 to 5, never falling along the last dimension, each value on 1 to 2048 neighbouring positions
Outputs:
- mixed: bfloat16 [4096, 3584], P(('seq', 'tensor'))
Inputs may be any that keep to these rules, and one draw needn't show every extreme that they name: `segments`: prompt ids never fall along the tokens, so each prompt's tokens are contiguous.
All inputs are finite; a program needn't handle non-finite values.
Results may differ from a plain program's by a relative error of at most 0.02.
Values may be sent and summed in bfloat16 or wider, within the bound.
A program may use at most 64 MiB of HBM per device.

v0:
```python
import jax
import jax.numpy as jnp
from jax import lax
from jax.sharding import PartitionSpec as P

BLOCK = 256
HIGHEST_PREC = lax.Precision.HIGHEST
NORM_EPS = 1e-05


def from_behind(block, axis, distance):
    devices = range(lax.axis_size(axis))
    route = [(i - distance, i) for i in devices if i - distance in devices]
    return lax.ppermute(block, axis, route)


def entering(array, axis, join, neutral):
    place = lax.axis_index(axis)
    gathered = jax.tree.map(
        lambda a, kind: lax.all_gather(a.astype(kind), axis),
        array,
        jax.tree.map(lambda a: jnp.bfloat16 if a.dtype == jnp.float32 else a.dtype, array),
    )
    state = jax.tree.map(lambda a, e: jnp.zeros_like(a) + jnp.asarray(e, a.dtype), array, neutral)

    def one(turn, state):
        return join(
            state,
            jax.tree.map(
                lambda a, own: lax.dynamic_index_in_dim(a, turn, 0, False).astype(own.dtype),
                gathered,
                array,
            ),
        )

    return lax.fori_loop(0, place, one, state)


def conv_tail(extended, seg_ext, taps, tok_rows):
    conv_len = taps.shape[0]
    seg_now = seg_ext[conv_len - 1 :]
    conv_sum = taps[conv_len - 1] * extended[conv_len - 1 :]
    for offset in range(1, conv_len):
        earlier = extended[conv_len - 1 - offset : conv_len - 1 - offset + tok_rows]
        seg_then = seg_ext[conv_len - 1 - offset : conv_len - 1 - offset + tok_rows]
        conv_sum = conv_sum + taps[conv_len - 1 - offset] * jnp.where(
            (seg_then == seg_now)[:, None], earlier, 0.0
        )
    return jax.nn.silu(conv_sum)


def ssd_block(carry, block):
    state, last_seg = carry
    inner_x, step_size, logdec, bmat, cmat, seg_ids = block
    cum_decay = jnp.cumsum(logdec, axis=0)
    position = jnp.arange(seg_ids.shape[0])
    visible = (seg_ids[:, None] == seg_ids[None, :]) & (position[:, None] >= position[None, :])
    gap_decay = jnp.where(
        visible[:, :, None], cum_decay[:, None, :] - cum_decay[None, :, :], -jnp.inf
    )
    scores = jnp.dot(cmat, bmat.T, precision=HIGHEST_PREC)
    weights = jnp.exp(gap_decay) * scores[:, :, None] * step_size[None, :, :]
    block_out = jnp.einsum("tsh,shp->thp", weights, inner_x, precision=HIGHEST_PREC)
    enter = jnp.where((seg_ids == last_seg)[:, None], jnp.exp(cum_decay), 0.0)
    block_out = block_out + enter[:, :, None] * jnp.einsum(
        "tn,hpn->thp", cmat, state, precision=HIGHEST_PREC
    )
    tail_weight = (
        jnp.where(
            (seg_ids == seg_ids[-1])[:, None], jnp.exp(cum_decay[-1][None, :] - cum_decay), 0.0
        )
        * step_size
    )
    carry_keep = jnp.where(seg_ids[-1] == last_seg, jnp.exp(cum_decay[-1]), 0.0)
    new_state = carry_keep[:, None, None] * state + jnp.einsum(
        "sh,shp,sn->hpn", tail_weight, inner_x, bmat, precision=HIGHEST_PREC
    )
    return ((new_state, seg_ids[-1]), block_out)


def link_states(earlier, later):
    gain_a, state_a, first_a, last_a = earlier
    gain_b, state_b, first_b, last_b = later
    joined = (first_b == last_a) | (last_a < 0.0) | (first_b < 0.0)
    passing = jnp.where(joined, gain_b, 0.0)
    merged_gain = gain_a * passing
    merged_state = passing[:, None, None] * state_a + state_b
    merged_first = jnp.where(first_a < 0.0, first_b, first_a)
    merged_last = jnp.where(last_b < 0.0, last_a, last_b)
    return (merged_gain, merged_state, merged_first, merged_last)


def local(
    tokens, w_zx, w_bc, w_dt, dt_bias, a_rate, d_skip, conv_x, conv_bc, norm_gain, w_out, segments
):
    tok_rows = tokens.shape[0]
    inner_w = w_zx.shape[2]
    heads = dt_bias.shape[0]
    head_size = inner_w // heads
    state_w = w_bc.shape[1] // 2
    rim_len = conv_x.shape[0] - 1
    piece = lax.all_gather(tokens, "tensor", axis=1, tiled=True)
    gate_rows = w_zx[0]
    inner_rows = w_zx[1]
    gate_sum = jnp.dot(piece, gate_rows, preferred_element_type=jnp.float32)
    inner_sum = jnp.dot(piece, inner_rows, preferred_element_type=jnp.float32)
    bc_sum = jnp.dot(piece, w_bc, preferred_element_type=jnp.float32)
    dt_raw = jnp.dot(piece, w_dt, preferred_element_type=jnp.float32)
    gate_proj = gate_sum.astype(jnp.bfloat16)
    inner_proj = inner_sum.astype(jnp.bfloat16)
    bc_proj = bc_sum.astype(jnp.bfloat16)
    rim_inner, rim_bc, rim_seg = from_behind(
        (
            inner_proj[tok_rows - rim_len :],
            bc_proj[tok_rows - rim_len :],
            segments[tok_rows - rim_len :].astype(jnp.bfloat16),
        ),
        "seq",
        1,
    )
    seg_ext = jnp.concatenate([rim_seg.astype(jnp.int32), segments], 0)
    conv_inner = conv_tail(
        jnp.concatenate([rim_inner.astype(jnp.float32), inner_proj.astype(jnp.float32)], 0),
        seg_ext,
        conv_x,
        tok_rows,
    )
    conv_state = conv_tail(
        jnp.concatenate([rim_bc.astype(jnp.float32), bc_proj.astype(jnp.float32)], 0),
        seg_ext,
        conv_bc,
        tok_rows,
    )
    bmat = conv_state[:, :state_w]
    cmat = conv_state[:, state_w:]
    step_size = jax.nn.softplus(dt_raw + dt_bias)
    logdec = -a_rate * step_size
    inner_heads = conv_inner.reshape(tok_rows, heads, head_size)
    nblocks = tok_rows // BLOCK
    blocks = (
        inner_heads.reshape(nblocks, BLOCK, heads, head_size),
        step_size.reshape(nblocks, BLOCK, heads),
        logdec.reshape(nblocks, BLOCK, heads),
        bmat.reshape(nblocks, BLOCK, state_w),
        cmat.reshape(nblocks, BLOCK, state_w),
        segments.reshape(nblocks, BLOCK),
    )
    start_carry = (jnp.zeros((heads, head_size, state_w), jnp.float32), jnp.array(-1, jnp.int32))
    (local_state, _), block_outs = lax.scan(ssd_block, start_carry, blocks)
    cum_device = jnp.cumsum(logdec, axis=0)
    device_gain = jnp.where(segments[0] == segments[-1], jnp.exp(cum_device[-1]), 0.0)
    seg_float = segments.astype(jnp.float32)
    element = (device_gain, local_state, seg_float[:1], seg_float[-1:])
    identity = (
        jnp.ones((heads,), jnp.float32),
        jnp.zeros_like(local_state),
        jnp.full((1,), -1.0, jnp.float32),
        jnp.full((1,), -1.0, jnp.float32),
    )
    incoming = entering(element, "seq", link_states, identity)
    state_in = incoming[1]
    last_in = incoming[3]
    enter = jnp.where((seg_float == last_in[0])[:, None], jnp.exp(cum_device), 0.0)
    ssd_out = block_outs.reshape(tok_rows, heads, head_size)
    ssd_out = ssd_out + enter[:, :, None] * jnp.einsum(
        "tn,hpn->thp", cmat, state_in, precision=HIGHEST_PREC
    )
    ssd_out = ssd_out + d_skip[None, :, None] * inner_heads
    gated = ssd_out.reshape(tok_rows, inner_w) * jax.nn.silu(gate_proj.astype(jnp.float32))
    local_squares = jnp.sum(gated * gated, axis=1)
    total_squares = lax.psum(local_squares, "tensor")
    scale = lax.rsqrt(total_squares / (inner_w * lax.axis_size("tensor")) + NORM_EPS)
    normed = (gated * scale[:, None] * norm_gain).astype(jnp.bfloat16)
    return lax.psum_scatter(
        jnp.dot(normed, w_out, preferred_element_type=jnp.float32).astype(jnp.bfloat16),
        "tensor",
        scatter_dimension=0,
        tiled=True,
    )


def solution(mesh):
    in_specs = (
        P("seq", "tensor"),
        P(None, None, "tensor"),
        P(),
        P(None, "tensor"),
        P("tensor"),
        P("tensor"),
        P("tensor"),
        P(None, "tensor"),
        P(),
        P("tensor"),
        P("tensor", None),
        P("seq"),
    )
    out_specs = P(("seq", "tensor"), None)
    return jax.shard_map(local, mesh=mesh, in_specs=in_specs, out_specs=out_specs, check_vma=False)
```

profile of v0, /device:TPU:8, one launch (start us, length us, event | category | flops | bytes accessed | tf_op | source)
XLA Modules:
  0.0 471.1 jit_solution(9409055045789982205)
XLA Ops:
  6.5 0.7 all-gather.6.cloned.1.call-update
  7.3 0.8 convert_convert_fusion
  8.2 1.3 dynamic-slice
  9.4 0.6 fusion.82
  10.0 1.4 dynamic-update-slice
  11.4 1.3 dynamic-update-slice.1
  12.7 1.9 collective-permute-start
  14.6 12.0 %all-reduce.2 = (bf16[8]{0:T(256)(128)(2,1)S(1)}, bf16[8]{0:T(256)(128)(2,1)S(1)}) all-reduce(bf16[8]{0:T(256)(128)(2,1)S(1)} %dynamic-update-slice, bf16[8]{0:T(256)(128)(2,1)S(1)} %dynamic-update-slice.1), channel_id=2, replica_groups=mesh['seq'=8,'tensor'=32] {'seq'}, use_global_device_ids=true, to_apply=%add | all-reduce | flops 16 | bytes 64
  26.6 0.7 reshape.139
  27.3 0.7 neg.20
  28.0 1.4 fusion.81
  30.7 0.8 slice_bitcast_fusion.8
  31.6 0.8 slice_bitcast_fusion.4
  32.4 0.8 pad_add_fusion
  33.2 0.8 slice_compare_fusion.2
  33.9 59.5 %all-gather.6.cloned.1.call-done = bf16[512,3584]{0,1:T(8,128)(2,1)} async-done(((bf16[512,112]{0,1:T(8,128)(2,1)}), bf16[512,3584]{0,1:T(8,128)(2,1)}) %all-gather.6.cloned.1.call-update) | async-done | bytes 3670032 | tf_op jit(solution)/shard_map/all_gather | solution.py:102
  93.4 2.7 broadcast_multiply_fusion
  96.3 3.6 fusion.83
  99.9 1.9 collective-permute-start.1
  101.8 1.1 fusion.84
  103.0 3.5 collective-permute-start.2
  106.6 0.6 reduce-window.16
  107.8 8.4 %all-gather.3 = bf16[8,1,2]{2,1,0:T(2,128)(2,1)S(1)} all-gather(bf16[1,1,2]{2,1,0:T(2,128)(2,1)S(1)} %bitcast.197), channel_id=1, replica_groups=mesh['seq'=8,'tensor'=32] {'seq'}, dimensions={0}, use_global_device_ids=true | all-gather | bytes 36 | tf_op jit(solution)/shard_map/all_gather | solution.py:20
  116.3 0.3 divide_multiply_fusion.1
  116.6 0.3 reshape.172
  117.3 0.3 divide_multiply_fusion
  118.0 16.2 %while.31 = (s32[]{:T(128)}, f32[2,64,64]{2,1,0:T(8,128)S(1)}, s32[]{:T(128)}, f32[2,256,2,64]{1,0,3,2:T(2,128)S(1)}, s32[2,256]{1,0:T(2,128)S(1)}, /*index=5*/f...) while((s32[]{:T(128)}, f32[2,64,64]{2,1,0:T(8,128)S(1)}, ...), condition=%wide.region_3.4_spmd.clone, body=%wide.region_0.3_spmd.clone.sunk | while | flops 202246672 | bytes 2326889 | solution.py:149
  118.0 0.6 reduce-window.26
  119.2 0.6 dynamic-slice.4
  119.8 0.6 broadcast_compare_fusion.3
  122.0 0.4 fusion.112
  122.6 0.8 fusion.114
  123.6 1.9 dynamic_update_slice.6
  126.1 0.6 reduce-window.26
  127.3 0.6 dynamic-slice.4
  127.9 0.6 broadcast_compare_fusion.3
  130.1 0.4 fusion.112
  130.7 0.8 fusion.114
  131.6 1.9 dynamic_update_slice.6
  134.4 11.6 %all-gather.1 = bf16[16,64,64]{2,1,0:T(8,128)(2,1)S(1)} all-gather(bf16[2,64,64]{2,1,0:T(8,128)(2,1)S(1)} %convert_element_type.85), channel_id=3, replica_groups=mesh['seq'=8,'tensor'=32] {'seq'}, dimensions={0}, use_global_device_ids=true | all-gather | bytes 147456 | tf_op jit(solution)/shard_map/all_gather | solution.py:20
  146.0 6.9 %while.30 = (s32[]{:T(128)}, f32[2,64,64]{2,1,0:T(8,128)S(1)}, f32[1]{0:T(128)}, s32[]{:T(128)}, bf16[8,1]{0,1:T(2,128)(2,1)S(1)}, /*index=5*/bf16[8,2]{0,1:T(2,...) while((s32[]{:T(128)}, f32[2,64,64]{2,1,0:T(8,128)S(1)}, ...), condition=%wide.region_7.8_spmd, body=%wide.region_6.7_spmd.sunk | while | flops 24592 | bytes 82183 | solution.py:36
  146.0 0.6 constant_dynamic-slice_fusion.7
  149.5 0.6 constant_dynamic-slice_fusion.7
  152.9 0.5 fusion.38
  153.6 3.5 multiply_reduce_fusion
  157.1 71.9 %psum.7 = f32[512]{0:T(512)S(1)} all-reduce(f32[512]{0:T(512)S(1)} %get-tuple-element.290), channel_id=1, replica_groups=mesh['seq'=8,'tensor'=32] {'tensor'}, use_global_device_ids=true, to_apply=%region_9.10 | all-reduce | flops 512 | bytes 4096 | tf_op jit(solution)/shard_map/psum | solution.py:171
  229.1 3.0 convolution_convert_fusion
  232.1 232.2 %reduce-scatter.2.cloned.1.call-done = bf16[16,3584]{1,0:T(8,128)(2,1)} async-done(((bf16[512,3584]{1,0:T(8,128)(2,1)}), bf16[16,3584]{1,0:T(8,128)(2,1)}) %reduce-scatter.2.cloned.1.call-update) | async-done | bytes 114704 | tf_op jit(solution)/shard_map/reduce_scatter | solution.py:174
  (93 shorter events, 6.4 us)
Async XLA Ops:
  6.5 222.5 %copy-start = (bf16[128,3584]{1,0:T(8,128)(2,1)S(1)}, bf16[128,3584]{1,0:T(8,128)(2,1)}, u32[]{:S(2)}) copy-start(bf16[128,3584]{1,0:T(8,128)(2,1)} %param.26) | copy-start | bytes 2752516
  6.5 86.9 %all-gather.6.cloned.1.call-start = ((), (), s32[]{:S(2)}) async-start(), calls=%async_computation.1 | async-start | bytes 3784704 | tf_op jit(solution)/shard_map/all_gather | solution.py:102
  7.3 457.0 %reduce-scatter.2.cloned.1.call-start = ((), (), s32[]{:S(2)}) async-start(), calls=%async_computation.2 | async-start | bytes 3784704 | tf_op jit(solution)/shard_map/reduce_scatter | solution.py:174
  12.7 19.7 %collective-permute-start = (bf16[3]{0:T(256)(128)(2,1)S(1)}, bf16[3]{0:T(256)(128)(2,1)S(1)}, u32[]{:S(2)}, u32[]{:S(2)}) collective-permute-start(bf16[3]{0:T(256)(128)(2,1)S(1)} %slice.118), channel_id=1, source_target_pairs={{0,32},{32,64},{64,96},{96,128},{128,160},{160,192},{192,224},{1,3... | collective-permute-start | bytes 26 | tf_op jit(solution)/shard_map/ppermute | solution.py:14
  96.1 5.7 %copy-start.2 = (bf16[3584,128]{1,0:T(8,128)(2,1)S(1)}, bf16[3584,128]{1,0:T(8,128)(2,1)}, u32[]{:S(2)}) copy-start(bf16[3584,128]{1,0:T(8,128)(2,1)} %param.18) | copy-start | bytes 2752516
  96.2 5.6 %copy-start.1 = (bf16[512,3584]{0,1:T(8,128)(2,1)S(1)}, bf16[512,3584]{0,1:T(8,128)(2,1)}, u32[]{:S(2)}) copy-start(bf16[512,3584]{0,1:T(8,128)(2,1)} %all-gather.6.cloned.1.call-done) | copy-start | bytes 11010052
  99.9 16.4 %collective-permute-start.1 = (bf16[3,128]{1,0:T(4,128)(2,1)S(1)}, bf16[3,128]{1,0:T(4,128)(2,1)S(1)}, u32[]{:S(2)}, u32[]{:S(2)}) collective-permute-start(bf16[3,128]{1,0:T(4,128)(2,1)S(1)} %slice.152), channel_id=1, source_target_pairs={{0,32},{32,64},{64,96},{96,128},{128,160},{160,192},{192,224},{1,3... | collective-permute-start | bytes 2312 | tf_op jit(solution)/shard_map/ppermute | solution.py:14
  103.0 14.3 %collective-permute-start.2 = (bf16[3,128]{1,0:T(4,128)(2,1)S(1)}, bf16[3,128]{1,0:T(4,128)(2,1)S(1)}, u32[]{:S(2)}, u32[]{:S(2)}) collective-permute-start(bf16[3,128]{1,0:T(4,128)(2,1)S(1)} %slice.157), channel_id=1, source_target_pairs={{0,32},{32,64},{64,96},{96,128},{128,160},{160,192},{192,224},{1,3... | collective-permute-start | bytes 2312 | tf_op jit(solution)/shard_map/ppermute | solution.py:14
  117.9 35.0 %copy-start.3 = (s32[512]{0:T(512)S(1)}, s32[512]{0:T(512)}, u32[]{:S(2)}) copy-start(s32[512]{0:T(512)} %param.27) | copy-start | bytes 6148
  117.9 35.0 %copy-start.5 = (f32[2]{0:T(128)S(1)}, f32[2]{0:T(128)}, u32[]{:S(2)}) copy-start(f32[2]{0:T(128)} %param.22) | copy-start | bytes 28
  153.5 75.6 %copy-start.4 = (f32[128]{0:T(128)S(1)}, f32[128]{0:T(128)}, u32[]{:S(2)}) copy-start(f32[128]{0:T(128)} %param.25) | copy-start | bytes 1540
Sparse Core Ops, SparseCore 0:
  9.9 83.4 all-gather.5
  232.2 232.0 reduce-scatter.1
where the time goes:
time: 472 us; the launch traced here: 471 us
  waiting for transfers between devices  292 us (62%)
  blocking collectives  104 us (22%)
  local copies, waits for them, and re-layouts  18.2 us (4%)
  matrix products  17.9 us (4%)
  between operations  15 us (3%)
  other arithmetic  8.35 us (2%)
  loops' own time  7.88 us (2%)
  starting transfers between devices  7.37 us (2%)
    reduce_scatter x1, waiting for transfers between devices, local(): lax.psum_scatter(jnp.dot(normed, w_out, preferred_element_type=jnp.float3...  232 us
    psum x1, blocking collectives, local(): total_squares = lax.psum(local_squares, 'tensor')  71.9 us
    all_gather x1, waiting for transfers between devices, local(): piece = lax.all_gather(tokens, 'tensor', axis=1, tiled=True)  59.5 us
    all_gather x2, blocking collectives, entering(): lax.all_gather(a.astype(kind), axis)  20 us
    unnamed x1, blocking collectives  12 us
  transfers between devices with their start and end apart: 5, of which 2 were waited for; matrix products, arithmetic and copies ran while one was open for 3% of the time, Pallas kernels for 0%

commit v1 on v0

--- a/solution.py
+++ b/solution.py
@@ -168,7 +168,7 @@
     ssd_out = ssd_out + d_skip[None, :, None] * inner_heads
     gated = ssd_out.reshape(tok_rows, inner_w) * jax.nn.silu(gate_proj.astype(jnp.float32))
     local_squares = jnp.sum(gated * gated, axis=1)
-    total_squares = lax.psum(local_squares, "tensor")
+    total_squares = jnp.sum(lax.all_gather(local_squares, "tensor"), axis=0)
     scale = lax.rsqrt(total_squares / (inner_w * lax.axis_size("tensor")) + NORM_EPS)
     normed = (gated * scale[:, None] * norm_gain).astype(jnp.bfloat16)
     return lax.psum_scatter(

time: 472 us -> 449 us (0.951)
  blocking collectives: 104 us -> 79.3 us
    psum x1 -> x0, blocking collectives: 71.9 us -> none  [local(): total_squares = lax.psum(local_squares, 'tensor')]
    all_gather x0 -> x1, blocking collectives: none -> 47.3 us  [local(): total_squares = jnp.sum(lax.all_gather(local_squares, 'tensor'), axis=0)]
where the time goes in v1:
time: 449 us; the launch traced here: 448 us
  waiting for transfers between devices  294 us (65%)
  blocking collectives  79.3 us (18%)
  local copies, waits for them, and re-layouts  18.2 us (4%)
  matrix products  17.9 us (4%)
  between operations  15 us (3%)
  other arithmetic  8.42 us (2%)
  loops' own time  7.88 us (2%)
  starting transfers between devices  7.37 us (2%)
    reduce_scatter x1, waiting for transfers between devices, local(): lax.psum_scatter(jnp.dot(normed, w_out, preferred_element_type=jnp.float3...  234 us
    all_gather x1, waiting for transfers between devices, local(): piece = lax.all_gather(tokens, 'tensor', axis=1, tiled=True)  59.5 us
    all_gather x1, blocking collectives, local(): total_squares = jnp.sum(lax.all_gather(local_squares, 'tensor'), axis=0)  47.3 us
    all_gather x2, blocking collectives, entering(): lax.all_gather(a.astype(kind), axis)  20 us
    unnamed x1, blocking collectives  12 us
  transfers between devices with their start and end apart: 5, of which 2 were waited for; matrix products, arithmetic and copies ran while one was open for 3% of the time, Pallas kernels for 0%

profile of v1, /device:TPU:8, one launch (start us, length us, event | category | flops | bytes accessed | tf_op | source)
XLA Modules:
  0.0 448.0 jit_solution(17487057363028681952)
XLA Ops:
  6.5 0.7 all-gather.8.cloned.1.call-update
  7.3 0.8 convert_convert_fusion
  8.2 1.3 dynamic-slice
  9.4 0.6 fusion.82
  10.0 1.4 dynamic-update-slice
  11.4 1.3 dynamic-update-slice.1
  12.7 1.9 collective-permute-start
  14.6 12.0 %all-reduce.2 = (bf16[8]{0:T(256)(128)(2,1)S(1)}, bf16[8]{0:T(256)(128)(2,1)S(1)}) all-reduce(bf16[8]{0:T(256)(128)(2,1)S(1)} %dynamic-update-slice, bf16[8]{0:T(256)(128)(2,1)S(1)} %dynamic-update-slice.1), channel_id=2, replica_groups=mesh['seq'=8,'tensor'=32] {'seq'}, use_global_device_ids=true, to_apply=%add | all-reduce | flops 16 | bytes 64
  26.6 0.7 reshape.143
  27.3 0.7 neg.20
  28.0 1.4 fusion.81
  30.7 0.8 slice_bitcast_fusion.8
  31.6 0.8 slice_bitcast_fusion.4
  32.4 0.8 pad_add_fusion
  33.2 0.8 slice_compare_fusion.2
  33.9 59.5 %all-gather.8.cloned.1.call-done = bf16[512,3584]{0,1:T(8,128)(2,1)} async-done(((bf16[512,112]{0,1:T(8,128)(2,1)}), bf16[512,3584]{0,1:T(8,128)(2,1)}) %all-gather.8.cloned.1.call-update) | async-done | bytes 3670032 | tf_op jit(solution)/shard_map/all_gather | solution.py:102
  93.4 2.7 broadcast_multiply_fusion
  96.3 3.6 fusion.83
  99.9 1.9 collective-permute-start.1
  101.8 1.1 fusion.84
  103.0 3.5 collective-permute-start.2
  106.6 0.6 reduce-window.16
  107.8 8.4 %all-gather.4 = bf16[8,1,2]{2,1,0:T(2,128)(2,1)S(1)} all-gather(bf16[1,1,2]{2,1,0:T(2,128)(2,1)S(1)} %bitcast.199), channel_id=1, replica_groups=mesh['seq'=8,'tensor'=32] {'seq'}, dimensions={0}, use_global_device_ids=true | all-gather | bytes 36 | tf_op jit(solution)/shard_map/all_gather | solution.py:20
  116.3 0.3 divide_multiply_fusion.1
  116.6 0.3 reshape.180
  117.3 0.3 divide_multiply_fusion
  118.0 16.2 %while.31 = (s32[]{:T(128)}, f32[2,64,64]{2,1,0:T(8,128)S(1)}, s32[]{:T(128)}, f32[2,256,2,64]{1,0,3,2:T(2,128)S(1)}, s32[2,256]{1,0:T(2,128)S(1)}, /*index=5*/f...) while((s32[]{:T(128)}, f32[2,64,64]{2,1,0:T(8,128)S(1)}, ...), condition=%wide.region_3.4_spmd.clone, body=%wide.region_0.3_spmd.clone.sunk | while | flops 202246672 | bytes 2326889 | solution.py:149
  118.0 0.6 reduce-window.26
  119.2 0.6 dynamic-slice.4
  119.8 0.6 broadcast_compare_fusion.3
  122.0 0.4 fusion.112
  122.6 0.8 fusion.114
  123.6 1.9 dynamic_update_slice.6
  126.1 0.6 reduce-window.26
  127.3 0.6 dynamic-slice.4
  127.9 0.6 broadcast_compare_fusion.3
  130.1 0.4 fusion.112
  130.7 0.8 fusion.114
  131.6 1.9 dynamic_update_slice.6
  134.4 11.6 %all-gather.1 = bf16[16,64,64]{2,1,0:T(8,128)(2,1)S(1)} all-gather(bf16[2,64,64]{2,1,0:T(8,128)(2,1)S(1)} %convert_element_type.85), channel_id=3, replica_groups=mesh['seq'=8,'tensor'=32] {'seq'}, dimensions={0}, use_global_device_ids=true | all-gather | bytes 147456 | tf_op jit(solution)/shard_map/all_gather | solution.py:20
  146.0 6.9 %while.30 = (s32[]{:T(128)}, f32[2,64,64]{2,1,0:T(8,128)S(1)}, f32[1]{0:T(128)}, s32[]{:T(128)}, bf16[8,1]{0,1:T(2,128)(2,1)S(1)}, /*index=5*/bf16[8,2]{0,1:T(2,...) while((s32[]{:T(128)}, f32[2,64,64]{2,1,0:T(8,128)S(1)}, ...), condition=%wide.region_7.8_spmd, body=%wide.region_6.7_spmd.sunk | while | flops 24592 | bytes 82183 | solution.py:36
  146.0 0.6 constant_dynamic-slice_fusion.7
  149.5 0.6 constant_dynamic-slice_fusion.7
  152.9 0.5 fusion.38
  153.6 3.5 multiply_reduce_fusion
  157.1 47.3 %all-gather.5 = f32[32,1,512]{2,1,0:T(1,128)S(1)} all-gather(f32[1,1,512]{2,1,0:T(1,128)S(1)} %bitcast.198), channel_id=5, replica_groups=mesh['seq'=8,'tensor'=32] {'tensor'}, dimensions={0}, use_global_device_ids=true | all-gather | bytes 67584 | tf_op jit(solution)/shard_map/all_gather | solution.py:171
  204.5 3.0 convolution_convert_fusion
  207.5 233.7 %reduce-scatter.2.cloned.1.call-done = bf16[16,3584]{1,0:T(8,128)(2,1)} async-done(((bf16[512,3584]{1,0:T(8,128)(2,1)}), bf16[16,3584]{1,0:T(8,128)(2,1)}) %reduce-scatter.2.cloned.1.call-update) | async-done | bytes 114704 | tf_op jit(solution)/shard_map/reduce_scatter | solution.py:174
  (94 shorter events, 6.5 us)
Async XLA Ops:
  6.5 198.0 %copy-start = (bf16[128,3584]{1,0:T(8,128)(2,1)S(1)}, bf16[128,3584]{1,0:T(8,128)(2,1)}, u32[]{:S(2)}) copy-start(bf16[128,3584]{1,0:T(8,128)(2,1)} %param.26) | copy-start | bytes 2752516
  6.5 86.9 %all-gather.8.cloned.1.call-start = ((), (), s32[]{:S(2)}) async-start(), calls=%async_computation.1 | async-start | bytes 3784704 | tf_op jit(solution)/shard_map/all_gather | solution.py:102
  7.3 433.9 %reduce-scatter.2.cloned.1.call-start = ((), (), s32[]{:S(2)}) async-start(), calls=%async_computation.2 | async-start | bytes 3784704 | tf_op jit(solution)/shard_map/reduce_scatter | solution.py:174
  12.7 19.7 %collective-permute-start = (bf16[3]{0:T(256)(128)(2,1)S(1)}, bf16[3]{0:T(256)(128)(2,1)S(1)}, u32[]{:S(2)}, u32[]{:S(2)}) collective-permute-start(bf16[3]{0:T(256)(128)(2,1)S(1)} %slice.118), channel_id=1, source_target_pairs={{0,32},{32,64},{64,96},{96,128},{128,160},{160,192},{192,224},{1,3... | collective-permute-start | bytes 26 | tf_op jit(solution)/shard_map/ppermute | solution.py:14
  96.1 5.7 %copy-start.2 = (bf16[3584,128]{1,0:T(8,128)(2,1)S(1)}, bf16[3584,128]{1,0:T(8,128)(2,1)}, u32[]{:S(2)}) copy-start(bf16[3584,128]{1,0:T(8,128)(2,1)} %param.18) | copy-start | bytes 2752516
  96.2 5.6 %copy-start.1 = (bf16[512,3584]{0,1:T(8,128)(2,1)S(1)}, bf16[512,3584]{0,1:T(8,128)(2,1)}, u32[]{:S(2)}) copy-start(bf16[512,3584]{0,1:T(8,128)(2,1)} %all-gather.8.cloned.1.call-done) | copy-start | bytes 11010052
  99.9 16.4 %collective-permute-start.1 = (bf16[3,128]{1,0:T(4,128)(2,1)S(1)}, bf16[3,128]{1,0:T(4,128)(2,1)S(1)}, u32[]{:S(2)}, u32[]{:S(2)}) collective-permute-start(bf16[3,128]{1,0:T(4,128)(2,1)S(1)} %slice.152), channel_id=1, source_target_pairs={{0,32},{32,64},{64,96},{96,128},{128,160},{160,192},{192,224},{1,3... | collective-permute-start | bytes 2312 | tf_op jit(solution)/shard_map/ppermute | solution.py:14
  103.0 14.3 %collective-permute-start.2 = (bf16[3,128]{1,0:T(4,128)(2,1)S(1)}, bf16[3,128]{1,0:T(4,128)(2,1)S(1)}, u32[]{:S(2)}, u32[]{:S(2)}) collective-permute-start(bf16[3,128]{1,0:T(4,128)(2,1)S(1)} %slice.157), channel_id=1, source_target_pairs={{0,32},{32,64},{64,96},{96,128},{128,160},{160,192},{192,224},{1,3... | collective-permute-start | bytes 2312 | tf_op jit(solution)/shard_map/ppermute | solution.py:14
  117.9 35.0 %copy-start.3 = (s32[512]{0:T(512)S(1)}, s32[512]{0:T(512)}, u32[]{:S(2)}) copy-start(s32[512]{0:T(512)} %param.27) | copy-start | bytes 6148
  117.9 35.0 %copy-start.5 = (f32[2]{0:T(128)S(1)}, f32[2]{0:T(128)}, u32[]{:S(2)}) copy-start(f32[2]{0:T(128)} %param.22) | copy-start | bytes 28
  153.5 51.1 %copy-start.4 = (f32[128]{0:T(128)S(1)}, f32[128]{0:T(128)}, u32[]{:S(2)}) copy-start(f32[128]{0:T(128)} %param.25) | copy-start | bytes 1540
Sparse Core Ops, SparseCore 0:
  9.9 83.4 all-gather.7
  207.6 233.4 reduce-scatter.1
